TPU v7x, 32 devices: a whole 2x2x4 slice. The times are simulated.
32 devices in a mesh: gx: 8 (over z, y), gy: 2 (over x), gz: 2 (over core).
Axes of the slice: x: 2, y: 2, z: 4, core: 2. Of those that a mesh axis runs over, the one named last changes fastest.
Arguments:
- populations: float32 [19, 64, 32, 256], P(None, 'gx', 'gy', 'gz'), as said below
- coarse_pops: float32 [19, 32, 16, 128], P(None, 'gx', 'gy', 'gz'), as said below
- fine_mask: int32 [64, 32, 256], P('gx', 'gy', 'gz'), may hold values 0 or 1
- coarse_mask: int32 [32, 16, 128], P('gx', 'gy', 'gz'), may hold values 0 or 1
- bead_data: float32 [8, 2, 2, 6, 512], P('gx', 'gy', 'gz'), as said below
- bead_bins: int32 [8, 2, 2, 1, 512], P('gx', 'gy', 'gz'), may hold values from -1 to 127, as said below
Outputs:
- fine_out: float32 [19, 64, 32, 256], P(None, 'gx', 'gy', 'gz')
- coarse_out: float32 [19, 32, 16, 128], P(None, 'gx', 'gy', 'gz')
Inputs may be any that keep to these rules, and one draw needn't show every extreme that they name: `populations`: populations are positive; rest population near 1/3, axis ones near 1/18, edge ones near 1/36, density within 0.5 to 1.7. `coarse_pops`: same law as populations on the coarse grid. `bead_bins`: in each source's block of 32 slots for one owner, the live slots come first; one owner receives 32 live slots from every source in every draw. `bead_data`: row 0 and 1 lie in -0.5 to 1.5, row 2 in -0.5 to 32 - 0.5; values in empty slots are arbitrary.
All inputs are finite; a program needn't handle non-finite values. No bound on the sum of `fine_mask` or of `coarse_mask` on one device may be relied on, other than what follows from the above.
Results may differ from a plain program's by a relative error of at most 0.0003.
Values sent between devices are 32-bit elements; how exact they have to be, the bound alone decides.
A program may use at most 128 MiB of HBM per device.

v0:
```python
import jax
import jax.numpy as jnp
import numpy as np
from jax import lax
from jax.sharding import PartitionSpec as P

BIN_Z = 32


VELOCITIES = np.array(
    [
        [0, 0, 0],
        [1, 0, 0],
        [-1, 0, 0],
        [0, 1, 0],
        [0, -1, 0],
        [0, 0, 1],
        [0, 0, -1],
        [1, 1, 0],
        [-1, -1, 0],
        [1, -1, 0],
        [-1, 1, 0],
        [1, 0, 1],
        [-1, 0, -1],
        [1, 0, -1],
        [-1, 0, 1],
        [0, 1, 1],
        [0, -1, -1],
        [0, 1, -1],
        [0, -1, 1],
    ]
)
LATTICE_WEIGHTS = np.array([1.0 / 3.0] + [1.0 / 18.0] * 6 + [1.0 / 36.0] * 12)
TAU_FINE = 1.2
TAU_COARSE = 0.85
TO_COARSE = 2.0 * TAU_COARSE / TAU_FINE
TO_FINE = TAU_FINE / (2.0 * TAU_COARSE)


def padded_2(value, sides, width):
    for axis, dim in sides:
        size, length = (lax.axis_size(axis), value.shape[dim])
        up = [(i, (i + 1) % size) for i in range(size)]
        down = [(j, i) for i, j in up]
        last = lax.slice_in_dim(value, length - width, length, axis=dim)
        leading = lax.slice_in_dim(value, 0, width, axis=dim)
        before = lax.ppermute(last, axis, up)
        after = lax.ppermute(leading, axis, down)
        value = jnp.concatenate([before, value, after], axis=dim)
    return value


def weights_like(field):
    return jnp.asarray(LATTICE_WEIGHTS, field.dtype).reshape((19,) + (1,) * (field.ndim - 1))


def moments(pops):
    table = jnp.asarray(VELOCITIES, pops.dtype)
    density = jnp.sum(pops, axis=0)
    momentum = jnp.tensordot(table.T, pops, axes=1, precision=lax.Precision.HIGHEST)
    return (density, momentum)


def equilibrium(density, velocity, like):
    table = jnp.asarray(VELOCITIES, like.dtype)
    along = jnp.tensordot(table, velocity, axes=1, precision=lax.Precision.HIGHEST)
    speed = jnp.sum(velocity * velocity, axis=0)
    return weights_like(like) * density * (1.0 + 3.0 * along + 4.5 * along * along - 1.5 * speed)


def rescale(pops, factor):
    density, momentum = moments(pops)
    balance = equilibrium(density, momentum / density, pops)
    return balance + factor * (pops - balance)


def collide(pops, force, tau):
    density, momentum = moments(pops)
    if force is None:
        velocity = momentum / density
        return pops - (pops - equilibrium(density, velocity, pops)) / tau
    table = jnp.asarray(VELOCITIES, pops.dtype)
    velocity = (momentum + 0.5 * force) / density
    balance = equilibrium(density, velocity, pops)
    along = jnp.tensordot(table, velocity, axes=1, precision=lax.Precision.HIGHEST)
    pushed = jnp.tensordot(table, force, axes=1, precision=lax.Precision.HIGHEST)
    work = jnp.sum(velocity * force, axis=0)
    source = (1.0 - 0.5 / tau) * weights_like(pops) * (3.0 * (pushed - work) + 9.0 * along * pushed)
    return pops - (pops - balance) / tau + source


def kernel_window(start, position, cells, span, live, dtype):
    index = jnp.arange(cells)[None, :]
    offset = index - start[:, None]
    inside = (offset >= 0) & (offset < span) & live[:, None]
    distance = offset.astype(dtype) - position[:, None]
    return jnp.where(inside, jnp.exp(-0.5 * distance * distance), jnp.zeros_like(distance))


def spread_beads(data, bins, cells_x, cells_y, cells_z):
    nby, nbz = (cells_y // 2, cells_z // BIN_Z)
    count = data.shape[1]
    live = bins >= 0
    safe = jnp.maximum(bins, 0).astype(jnp.int32)
    block_x = safe // (nby * nbz)
    block_y = safe // nbz % nby
    block_z = safe % nbz
    kernel_x = kernel_window(2 * block_x, data[0], cells_x, 2, live, data.dtype)
    kernel_y = kernel_window(2 * block_y, data[1], cells_y, 2, live, data.dtype)
    kernel_z = kernel_window(BIN_Z * block_z, data[2], cells_z, BIN_Z, live, data.dtype)
    plane = (kernel_x[:, :, None] * kernel_y[:, None, :]).reshape(count, cells_x * cells_y)
    loaded = (data[3:6].T[:, :, None] * plane[:, None, :]).reshape(count, 3 * cells_x * cells_y)
    summed = lax.dot_general(
        loaded, kernel_z, (((0,), (0,)), ((), ())), precision=lax.Precision.HIGHEST
    )
    return summed.reshape(3, cells_x, cells_y, cells_z)


def expand_parent(parent):
    q, a, b, c = parent.shape
    grown = jnp.broadcast_to(parent[:, :, None, :, None, :, None], (q, a, 2, b, 2, c, 2))
    return grown.reshape(q, 2 * a, 2 * b, 2 * c)


def from_padded(padded, sizes):
    moved = []
    for i in range(19):
        start = [1 - int(v) for v in VELOCITIES[i]]
        moved.append(
            padded[
                i,
                start[0] : start[0] + sizes[0],
                start[1] : start[1] + sizes[1],
                start[2] : start[2] + sizes[2],
            ]
        )
    return jnp.stack(moved)


def local(populations, coarse_pops, fine_mask, coarse_mask, bead_data, bead_bins):
    cells_x, cells_y, cells_z = (populations.shape[1], populations.shape[2], populations.shape[3])
    half_x, half_y, half_z = (cells_x // 2, cells_y // 2, cells_z // 2)
    width_gx = lax.axis_size("gx")
    width_gy = lax.axis_size("gy")
    slots = bead_data.shape[4] // (width_gx * width_gy)
    sectioned = bead_data.reshape(1, 1, 1, 6, width_gx, width_gy, slots)
    sectioned_bins = bead_bins.reshape(1, 1, 1, 1, width_gx, width_gy, slots)
    arrived, arrived_bins = (
        lax.all_to_all(
            lax.all_to_all(sectioned, "gx", split_axis=4, concat_axis=4, tiled=True),
            "gy",
            split_axis=5,
            concat_axis=5,
            tiled=True,
        ),
        lax.all_to_all(
            lax.all_to_all(sectioned_bins, "gx", split_axis=4, concat_axis=4, tiled=True),
            "gy",
            split_axis=5,
            concat_axis=5,
            tiled=True,
        ),
    )
    force = spread_beads(
        arrived.reshape(6, -1), arrived_bins.reshape(-1), cells_x, cells_y, cells_z
    )
    restricted = populations.reshape(19, half_x, 2, half_y, 2, half_z, 2).mean(axis=(2, 4, 6))
    coarse_pre = jnp.where(coarse_mask[None] == 1, rescale(restricted, TO_COARSE), coarse_pops)
    parent = expand_parent(rescale(coarse_pre, TO_FINE))
    fine_pre = jnp.where(fine_mask[None] == 1, populations, parent)
    fine_post = collide(fine_pre, force, TAU_FINE)
    padded = padded_2(fine_post, (("gx", 1), ("gy", 2), ("gz", 3)), 1)
    fine_out = from_padded(padded, (cells_x, cells_y, cells_z))
    coarse_post = collide(coarse_pre, None, TAU_COARSE)
    padded = padded_2(coarse_post, (("gx", 1), ("gy", 2), ("gz", 3)), 1)
    coarse_out = from_padded(padded, (half_x, half_y, half_z))
    return (fine_out, coarse_out)


def solution(mesh):
    in_specs = (
        P(None, "gx", "gy", "gz"),
        P(None, "gx", "gy", "gz"),
        P("gx", "gy", "gz"),
        P("gx", "gy", "gz"),
        P("gx", "gy", "gz", None, None),
        P("gx", "gy", "gz", None, None),
    )
    out_specs = (P(None, "gx", "gy", "gz"), P(None, "gx", "gy", "gz"))
    return jax.shard_map(local, mesh=mesh, in_specs=in_specs, out_specs=out_specs, check_vma=False)
```

profile of v0, /device:TPU:0, one launch (start us, length us, event | category | flops | bytes accessed | tf_op | source)
XLA Modules:
  0.0 141.6 jit_solution(10945640419669381526)
XLA Ops:
  0.6 6.2 %copy.63 = f32[19,8,16,128]{0,3,2,1:T(8,128)} copy(f32[19,8,16,128]{3,2,1,0:T(8,128)} %param.20) | data formatting | bytes 2490368 | tf_op args[0]
  6.8 8.7 %reduce_sum.85 = f32[19,4,8,64]{0,3,2,1:T(8,128)S(1)} reduce(f32[19,4,2,8,2,64,2]{0,6,5,4,3,2,1:T(2,128)} %bitcast.56, f32[]{:T(128)} %constant.45.clone.1), dimensions={2,4,6}, to_apply=%region_0.1 | reduce | flops 272384 | bytes 1400836 | tf_op jit(solution)/shard_map/reduce_sum | solution.py:167
  19.3 3.0 %collective-permute-start.6 = (f32[19,1,8,64]{3,0,2,1:T(8,128)}, f32[19,1,8,64]{3,0,2,1:T(8,128)}, u32[]{:S(2)}, u32[]{:S(2)}) collective-permute-start(f32[19,1,8,64]{3,0,2,1:T(8,128)} %get-tuple-element.63), channel_id=1, source_target_pairs={{0,4},{4,8},{8,12},{12,16},{16,20},{20,24},{24,28},{28,0},{1,5},{5... | collective-permute-start | bytes 116744 | tf_op jit(solution)/shard_map/ppermute | solution.py:47
  22.3 3.0 %collective-permute-start.7 = (f32[19,1,8,64]{3,0,2,1:T(8,128)}, f32[19,1,8,64]{3,0,2,1:T(8,128)}, u32[]{:S(2)}, u32[]{:S(2)}) collective-permute-start(f32[19,1,8,64]{3,0,2,1:T(8,128)} %get-tuple-element.62), channel_id=1, source_target_pairs={{4,0},{8,4},{12,8},{16,12},{20,16},{24,20},{28,24},{0,28},{5,1},{9... | collective-permute-start | bytes 116744 | tf_op jit(solution)/shard_map/ppermute | solution.py:48
  27.2 3.3 %all-to-all-start.2 = ((s32[1,1,1,1,8,2,32]{6,5,3,2,1,0,4:T(2,128)}), s32[1,1,1,1,8,2,32]{6,5,3,2,1,0,4:T(2,128)S(1)}, u32[]{:S(2)}, u32[]{:S(2)}) async-start(s32[1,1,1,1,8,2,32]{6,5,3,2,1,0,4:T(2,128)} %reshape.263), calls=%async_computation.2 | async-start | bytes 16384 | tf_op jit(solution)/shard_map/all_to_all | solution.py:157
  31.0 7.5 %broadcast_in_dim.20 = f32[19,4,2,8,2,64,2]{0,6,5,4,3,2,1:T(2,128)} broadcast(f32[19,4,8,64]{0,3,2,1:T(8,128)S(1)} %copy.66), dimensions={0,1,3,5} | broadcast | bytes 1400832 | tf_op jit(solution)/shard_map/broadcast_in_dim | solution.py:121
  38.4 5.3 %copy.68 = f32[19,8,16,128]{3,0,2,1:T(8,128)S(1)} copy(f32[19,8,16,128]{0,3,2,1:T(8,128)} %bitcast.57) | data formatting | bytes 2490368 | tf_op jit(solution)/shard_map/reshape | solution.py:122
  44.5 3.4 %all-to-all-start.3 = ((s32[2,1,256]{2,1,0:T(1,128)}), s32[2,1,256]{2,1,0:T(1,128)S(1)}, u32[]{:S(2)}, u32[]{:S(2)}) async-start(s32[2,1,256]{2,1,0:T(1,128)} %reshape.280), calls=%async_computation.3 | async-start | bytes 4096 | tf_op jit(solution)/shard_map/all_to_all | solution.py:156
  51.3 6.0 %all-to-all-start = ((f32[8,1,384]{2,1,0:T(1,128)}), f32[8,1,384]{2,1,0:T(1,128)S(1)}, u32[]{:S(2)}, u32[]{:S(2)}) async-start(f32[8,1,384]{2,1,0:T(1,128)} %reshape.276), calls=%async_computation | async-start | bytes 24576 | tf_op jit(solution)/shard_map/all_to_all | solution.py:150
  59.1 4.7 %all-to-all-done = f32[8,1,384]{2,1,0:T(1,128)S(1)} async-done(((f32[8,1,384]{2,1,0:T(1,128)}), f32[8,1,384]{2,1,0:T(1,128)S(1)}, u32[]{:S(2)}, u32[]{:S(2)}) %all-to-all-start) | async-done | bytes 12320 | tf_op jit(solution)/shard_map/all_to_all | solution.py:150
  65.9 3.2 %all-to-all-start.1 = ((f32[2,1,1536]{2,1,0:T(1,128)}), f32[2,1,1536]{2,1,0:T(1,128)S(1)}, u32[]{:S(2)}, u32[]{:S(2)}) async-start(f32[2,1,1536]{2,1,0:T(1,128)} %reshape.278), calls=%async_computation.1 | async-start | bytes 24576 | tf_op jit(solution)/shard_map/all_to_all | solution.py:149
  69.9 3.1 %all-to-all-done.1 = f32[2,1,1536]{2,1,0:T(1,128)S(1)} async-done(((f32[2,1,1536]{2,1,0:T(1,128)}), f32[2,1,1536]{2,1,0:T(1,128)S(1)}, u32[]{:S(2)}, u32[]{:S(2)}) %all-to-all-start.1) | async-done | bytes 12320 | tf_op jit(solution)/shard_map/all_to_all | solution.py:149
  78.0 2.1 %fusion.18 = f32[8,16,128,19]{2,3,1,0:T(8,128)S(1)} fusion(f32[19,3,1,1]{0,1,3,2:T(4,128)} %constant.118, f32[3,8,16,128]{3,2,1,0:T(8,128)S(1)} %fusion.24), kind=kOutput, calls=%fused_computation.35 | convolution fusion | flops 11206656 | bytes 1442020 | tf_op jit(solution)/shard_map/dot_general | solution.py:86
  82.2 3.6 %fusion.6 = f32[19,8,16,128]{3,0,2,1:T(8,128)S(1)} fusion(f32[8,16,128,19]{2,3,1,0:T(8,128)S(1)} %fusion.18, f32[3,8,16,128]{3,0,2,1:T(4,128)S(1)} %get-tuple-element.82, f32[19,3,1,1]{0,1,3,2:T(4,128)S(1)} %copy-done.9, f32[19]{0:T(128)S(1)} %copy-done.15, f32[8,16,128]{2,1,0:T(8,128)S(1)} %get-tuple-element.11, ...), kind=kOutput, calls=%fused_computation.8 | convolution fusion | flops 17121280 | bytes 5390716 | tf_op jit(solution)/shard_map/dot_general | solution.py:66
  89.9 4.2 %collective-permute-start.1 = (f32[19,1,16,128]{3,0,2,1:T(8,128)S(1)}, f32[19,1,16,128]{3,0,2,1:T(8,128)S(1)}, u32[]{:S(2)}, u32[]{:S(2)}) collective-permute-start(f32[19,1,16,128]{3,0,2,1:T(8,128)S(1)} %get-tuple-element.35), channel_id=1, source_target_pairs={{4,0},{8,4},{12,8},{16,12},{20,16},{24,20},{28,24},{0,28},{5,1},{9... | collective-permute-start | bytes 466952 | tf_op jit(solution)/shard_map/ppermute | solution.py:48
  110.9 2.8 %stack.7 = f32[19,4,8,64]{3,0,2,1:T(8,128)S(1)} concatenate(f32[1,4,8,64]{3,0,2,1:T(1,128)S(1)} %get-tuple-element.61, f32[1,4,8,64]{3,0,2,1:T(1,128)} %get-tuple-element.59, f32[1,4,8,64]{3,0,2,1:T(1,128)} %get-tuple-element.60, f32[1,4,8,64]{3,0,2,1:T(1,128)} %get-tuple-element.56, f32[1,4,8,64]{3,0,2,1:T(1,128)} %get-tuple-element.55, f32[1,4,8,64]{3,0,2,1:T(1,128)} %get-tuple-element.46, ...), dimensions={0} | concatenate | bytes 311296 | tf_op jit(solution)/shard_map/stack | solution.py:137
  115.4 2.7 %fusion.64 = (f32[19,10,18,1]{3,0,2,1:T(8,128)}, f32[19,10,18,1]{3,0,2,1:T(8,128)}) fusion(f32[19,10,18,128]{3,0,2,1:T(8,128)S(1)} %pad_maximum_fusion), kind=kLoop, calls=%fused_computation.172 | loop fusion | bytes 54720 | tf_op jit(solution)/shard_map/slice | solution.py:46
  118.1 2.8 %copy.87 = f32[19,10,18,1]{0,3,2,1:T(1,128)S(1)} copy(f32[19,10,18,1]{3,0,2,1:T(8,128)} %get-tuple-element.22) | data formatting | bytes 27360 | tf_op jit(solution)/shard_map/slice | solution.py:46
  120.9 2.8 %copy.85 = f32[19,10,18,1]{0,3,2,1:T(1,128)S(1)} copy(f32[19,10,18,1]{3,0,2,1:T(8,128)} %get-tuple-element.23) | data formatting | bytes 27360 | tf_op jit(solution)/shard_map/slice | solution.py:45
  125.1 2.6 %copy.88 = f32[19,10,18,1]{3,0,2,1:T(8,128)} copy(f32[19,10,18,1]{0,3,2,1:T(1,128)S(1)} %collective-permute-done.5) | data formatting | bytes 27360 | tf_op jit(solution)/shard_map/ppermute | solution.py:48
  127.6 2.4 %pad_maximum_fusion.22 = (f32[1,8,16,128]{3,0,2,1:T(1,128)S(1)}, f32[1,8,16,128]{3,0,2,1:T(1,128)S(1)}, f32[1,8,16,128]{3,0,2,1:T(1,128)S(1)}, f32[1,8,16,128]{3,0,2,1:T(1,128)S(1)}) fusion(f32[19,10,18,1]{3,0,2,1:T(8,128)} %copy.88, f32[19,10,1,128]{3,0,2,1:T(8,128)S(1)} %collective-permute-done.3, f32[19,10,1,128]{3,0,2,1:T(8,128)S(1)} %collective-permute-done.2, ...), kind=kLoop, calls=%fused_computation.80 | loop fusion | flops 229376 | bytes 2026864 | tf_op jit(solution)/shard_map/slice | solution.py:130
  130.9 2.6 %copy.86 = f32[19,10,18,1]{3,0,2,1:T(8,128)} copy(f32[19,10,18,1]{0,3,2,1:T(1,128)S(1)} %collective-permute-done.4) | data formatting | bytes 27360 | tf_op jit(solution)/shard_map/ppermute | solution.py:47
  133.5 2.1 %pad_maximum_fusion.23 = (f32[1,8,16,128]{3,0,2,1:T(1,128)S(1)}, f32[1,8,16,128]{3,0,2,1:T(1,128)S(1)}, f32[1,8,16,128]{3,0,2,1:T(1,128)S(1)}, f32[1,8,16,128]{3,0,2,1:T(1,128)S(1)}) fusion(f32[19,10,18,1]{3,0,2,1:T(8,128)} %copy.86, f32[19,10,1,128]{3,0,2,1:T(8,128)S(1)} %collective-permute-done.3, f32[19,10,1,128]{3,0,2,1:T(8,128)S(1)} %collective-permute-done.2, ...), kind=kLoop, calls=%fused_computation.81 | loop fusion | flops 229376 | bytes 2026864 | tf_op jit(solution)/shard_map/slice | solution.py:130
  136.9 3.5 %stack.6 = f32[19,8,16,128]{3,0,2,1:T(8,128)S(1)} concatenate(f32[1,8,16,128]{3,0,2,1:T(1,128)} %get-tuple-element.34, f32[1,8,16,128]{3,0,2,1:T(1,128)S(1)} %get-tuple-element.32, f32[1,8,16,128]{3,0,2,1:T(1,128)S(1)} %get-tuple-element.33, f32[1,8,16,128]{3,0,2,1:T(1,128)} %get-tuple-element.29, f32[1,8,16,128]{3,0,2,1:T(1,128)} %get-tuple-element.28, ...), dimensions={0} | concatenate | bytes 2490368 | tf_op jit(solution)/shard_map/stack | solution.py:137
  (139 shorter events, 49.0 us)
Async XLA Ops:
  16.6 9.3 %copy-start.11 = (s32[1,1,1,1,512]{4,3,2,1,0:T(1,128)S(1)}, s32[1,1,1,1,512]{4,3,2,1,0:T(1,128)}, u32[]{:S(2)}) copy-start(s32[1,1,1,1,512]{4,3,2,1,0:T(1,128)} %param.25) | copy-start | bytes 6148
  16.6 13.9 %copy-start.5 = (s32[8,16,128]{2,1,0:T(8,128)S(1)}, s32[8,16,128]{2,1,0:T(8,128)}, u32[]{:S(2)}) copy-start(s32[8,16,128]{2,1,0:T(8,128)} %param.22) | copy-start | bytes 196612
  19.3 66.5 %collective-permute-start.6 = (f32[19,1,8,64]{3,0,2,1:T(8,128)}, f32[19,1,8,64]{3,0,2,1:T(8,128)}, u32[]{:S(2)}, u32[]{:S(2)}) collective-permute-start(f32[19,1,8,64]{3,0,2,1:T(8,128)} %get-tuple-element.63), channel_id=1, source_target_pairs={{0,4},{4,8},{8,12},{12,16},{16,20},{20,24},{24,28},{28,0},{1,5},{5... | collective-permute-start | bytes 116744 | tf_op jit(solution)/shard_map/ppermute | solution.py:47
  22.3 63.5 %collective-permute-start.7 = (f32[19,1,8,64]{3,0,2,1:T(8,128)}, f32[19,1,8,64]{3,0,2,1:T(8,128)}, u32[]{:S(2)}, u32[]{:S(2)}) collective-permute-start(f32[19,1,8,64]{3,0,2,1:T(8,128)} %get-tuple-element.62), channel_id=1, source_target_pairs={{4,0},{8,4},{12,8},{16,12},{20,16},{24,20},{28,24},{0,28},{5,1},{9... | collective-permute-start | bytes 116744 | tf_op jit(solution)/shard_map/ppermute | solution.py:48
  27.2 16.6 %all-to-all-start.2 = ((s32[1,1,1,1,8,2,32]{6,5,3,2,1,0,4:T(2,128)}), s32[1,1,1,1,8,2,32]{6,5,3,2,1,0,4:T(2,128)S(1)}, u32[]{:S(2)}, u32[]{:S(2)}) async-start(s32[1,1,1,1,8,2,32]{6,5,3,2,1,0,4:T(2,128)} %reshape.263), calls=%async_computation.2 | async-start | bytes 16384 | tf_op jit(solution)/shard_map/all_to_all | solution.py:157
  38.4 9.4 %copy-start.2 = (f32[19,8,16,128]{3,2,1,0:T(8,128)S(1)}, f32[19,8,16,128]{3,2,1,0:T(8,128)}, u32[]{:S(2)}) copy-start(f32[19,8,16,128]{3,2,1,0:T(8,128)} %param.20) | copy-start | bytes 3735556
  43.8 5.2 %copy-start.7 = (f32[1,1,1,6,512]{4,2,3,1,0:T(1,128)S(1)}, f32[1,1,1,6,512]{4,2,3,1,0:T(1,128)}, u32[]{:S(2)}) copy-start(f32[1,1,1,6,512]{4,2,3,1,0:T(1,128)} %param.24) | copy-start | bytes 36868
  44.5 6.8 %all-to-all-start.3 = ((s32[2,1,256]{2,1,0:T(1,128)}), s32[2,1,256]{2,1,0:T(1,128)S(1)}, u32[]{:S(2)}, u32[]{:S(2)}) async-start(s32[2,1,256]{2,1,0:T(1,128)} %reshape.280), calls=%async_computation.3 | async-start | bytes 4096 | tf_op jit(solution)/shard_map/all_to_all | solution.py:156
  49.0 31.1 %copy-start.4 = (f32[8,16,128]{2,1,0:T(8,128)}, f32[8,16,128]{2,1,0:T(8,128)S(1)}, u32[]{:S(2)}) copy-start(f32[8,16,128]{2,1,0:T(8,128)S(1)} %fusion.63) | copy-start | bytes 196612
  51.3 12.5 %all-to-all-start = ((f32[8,1,384]{2,1,0:T(1,128)}), f32[8,1,384]{2,1,0:T(1,128)S(1)}, u32[]{:S(2)}, u32[]{:S(2)}) async-start(f32[8,1,384]{2,1,0:T(1,128)} %reshape.276), calls=%async_computation | async-start | bytes 24576 | tf_op jit(solution)/shard_map/all_to_all | solution.py:150
  65.9 7.1 %all-to-all-start.1 = ((f32[2,1,1536]{2,1,0:T(1,128)}), f32[2,1,1536]{2,1,0:T(1,128)S(1)}, u32[]{:S(2)}, u32[]{:S(2)}) async-start(f32[2,1,1536]{2,1,0:T(1,128)} %reshape.278), calls=%async_computation.1 | async-start | bytes 24576 | tf_op jit(solution)/shard_map/all_to_all | solution.py:149
  69.9 5.6 %copy-start.10 = (pred[512]{0:T(512)(128)(4,1)}, pred[512]{0:T(512)(128)(4,1)S(1)}, u32[]{:S(2)}) copy-start(pred[512]{0:T(512)(128)(4,1)S(1)} %ge.39) | copy-start | bytes 1540
  76.3 3.8 %copy-start.9 = (f32[19,3,1,1]{0,1,3,2:T(4,128)S(1)}, f32[19,3,1,1]{0,1,3,2:T(4,128)}, u32[]{:S(2)}) copy-start(f32[19,3,1,1]{0,1,3,2:T(4,128)} %constant.118) | copy-start | bytes 688
  86.6 7.5 %collective-permute-start.8 = (f32[19,6,1,64]{3,0,2,1:T(8,128)S(1)}, f32[19,6,1,64]{3,0,2,1:T(8,128)S(1)}, u32[]{:S(2)}, u32[]{:S(2)}) collective-permute-start(f32[19,6,1,64]{3,0,2,1:T(8,128)S(1)} %get-tuple-element.58), channel_id=1, source_target_pairs={{0,2},{2,0},{1,3},{3,1},{4,6},{6,4},{5,7},{7,5},{8,10},{10,8},{9,1... | collective-permute-start | bytes 87560 | tf_op jit(solution)/shard_map/ppermute | solution.py:47
  86.7 7.4 %collective-permute-start.9 = (f32[19,6,1,64]{3,0,2,1:T(8,128)S(1)}, f32[19,6,1,64]{3,0,2,1:T(8,128)S(1)}, u32[]{:S(2)}, u32[]{:S(2)}) collective-permute-start(f32[19,6,1,64]{3,0,2,1:T(8,128)S(1)} %get-tuple-element.57), channel_id=1, source_target_pairs={{2,0},{0,2},{3,1},{1,3},{6,4},{4,6},{7,5},{5,7},{10,8},{8,10},{11,... | collective-permute-start | bytes 87560 | tf_op jit(solution)/shard_map/ppermute | solution.py:48
  89.4 17.0 %collective-permute-start = (f32[19,1,16,128]{3,0,2,1:T(8,128)}, f32[19,1,16,128]{3,0,2,1:T(8,128)S(1)}, u32[]{:S(2)}, u32[]{:S(2)}) collective-permute-start(f32[19,1,16,128]{3,0,2,1:T(8,128)} %get-tuple-element.36), channel_id=1, source_target_pairs={{0,4},{4,8},{8,12},{12,16},{16,20},{20,24},{24,28},{28,0},{1,5},{5... | collective-permute-start | bytes 466952 | tf_op jit(solution)/shard_map/ppermute | solution.py:47
  89.9 16.5 %collective-permute-start.1 = (f32[19,1,16,128]{3,0,2,1:T(8,128)S(1)}, f32[19,1,16,128]{3,0,2,1:T(8,128)S(1)}, u32[]{:S(2)}, u32[]{:S(2)}) collective-permute-start(f32[19,1,16,128]{3,0,2,1:T(8,128)S(1)} %get-tuple-element.35), channel_id=1, source_target_pairs={{4,0},{8,4},{12,8},{16,12},{20,16},{24,20},{28,24},{0,28},{5,1},{9... | collective-permute-start | bytes 466952 | tf_op jit(solution)/shard_map/ppermute | solution.py:48
  97.7 5.8 %collective-permute-start.11 = (f32[19,6,10,1]{0,3,2,1:T(1,128)S(1)}, f32[19,6,10,1]{0,3,2,1:T(1,128)}, u32[]{:S(2)}, u32[]{:S(2)}) collective-permute-start(f32[19,6,10,1]{0,3,2,1:T(1,128)S(1)} %copy.91), channel_id=1, source_target_pairs={{1,0},{0,1},{3,2},{2,3},{5,4},{4,5},{7,6},{6,7},{9,8},{8,9},{11,10... | collective-permute-start | bytes 13688 | tf_op jit(solution)/shard_map/ppermute | solution.py:48
  98.3 2.0 %collective-permute-start.10 = (f32[19,6,10,1]{0,3,2,1:T(1,128)S(1)}, f32[19,6,10,1]{0,3,2,1:T(1,128)S(1)}, u32[]{:S(2)}, u32[]{:S(2)}) collective-permute-start(f32[19,6,10,1]{0,3,2,1:T(1,128)S(1)} %copy.89), channel_id=1, source_target_pairs={{0,1},{1,0},{2,3},{3,2},{4,5},{5,4},{6,7},{7,6},{8,9},{9,8},{10,11... | collective-permute-start | bytes 13688 | tf_op jit(solution)/shard_map/ppermute | solution.py:47
  107.1 7.4 %collective-permute-start.2 = (f32[19,10,1,128]{3,0,2,1:T(8,128)}, f32[19,10,1,128]{3,0,2,1:T(8,128)S(1)}, u32[]{:S(2)}, u32[]{:S(2)}) collective-permute-start(f32[19,10,1,128]{3,0,2,1:T(8,128)} %get-tuple-element.31), channel_id=1, source_target_pairs={{0,2},{2,0},{1,3},{3,1},{4,6},{6,4},{5,7},{7,5},{8,10},{10,8},{9,1... | collective-permute-start | bytes 291848 | tf_op jit(solution)/shard_map/ppermute | solution.py:47
  107.2 8.0 %collective-permute-start.3 = (f32[19,10,1,128]{3,0,2,1:T(8,128)}, f32[19,10,1,128]{3,0,2,1:T(8,128)S(1)}, u32[]{:S(2)}, u32[]{:S(2)}) collective-permute-start(f32[19,10,1,128]{3,0,2,1:T(8,128)} %get-tuple-element.30), channel_id=1, source_target_pairs={{2,0},{0,2},{3,1},{1,3},{6,4},{4,6},{7,5},{5,7},{10,8},{8,10},{11,... | collective-permute-start | bytes 291848 | tf_op jit(solution)/shard_map/ppermute | solution.py:48
  120.9 4.2 %collective-permute-start.5 = (f32[19,10,18,1]{0,3,2,1:T(1,128)S(1)}, f32[19,10,18,1]{0,3,2,1:T(1,128)S(1)}, u32[]{:S(2)}, u32[]{:S(2)}) collective-permute-start(f32[19,10,18,1]{0,3,2,1:T(1,128)S(1)} %copy.87), channel_id=1, source_target_pairs={{1,0},{0,1},{3,2},{2,3},{5,4},{4,5},{7,6},{6,7},{9,8},{8,9},{11,10... | collective-permute-start | bytes 41048 | tf_op jit(solution)/shard_map/ppermute | solution.py:48
  123.7 7.2 %collective-permute-start.4 = (f32[19,10,18,1]{0,3,2,1:T(1,128)S(1)}, f32[19,10,18,1]{0,3,2,1:T(1,128)S(1)}, u32[]{:S(2)}, u32[]{:S(2)}) collective-permute-start(f32[19,10,18,1]{0,3,2,1:T(1,128)S(1)} %copy.85), channel_id=1, source_target_pairs={{0,1},{1,0},{2,3},{3,2},{4,5},{5,4},{6,7},{7,6},{8,9},{9,8},{10,11... | collective-permute-start | bytes 41048 | tf_op jit(solution)/shard_map/ppermute | solution.py:47
  127.6 2.4 %copy-start.1 = (f32[19,10,18,1]{3,0,2,1:T(8,128)S(1)}, f32[19,10,18,1]{3,0,2,1:T(8,128)}, u32[]{:S(2)}) copy-start(f32[19,10,18,1]{3,0,2,1:T(8,128)} %copy.88) | copy-start | bytes 41044
  (8 other events, 12.4 us)
where the time goes:
time: 143 us; the launch traced here: 142 us
  local copies, waits for them, and re-layouts  55 us (38%)
  starting transfers between devices  31.9 us (22%)
  other arithmetic  31.8 us (22%)
  matrix products  11.7 us (8%)
  waiting for transfers between devices  10 us (7%)
    unnamed x42, local copies, waits for them, and re-layouts  11.4 us
    ppermute x6, starting transfers between devices, padded_2(): after = lax.ppermute(leading, axis, down)  11.3 us
    concatenate x10, other arithmetic, padded_2(): value = jnp.concatenate([before, value, after], axis=dim)  9.82 us
    slice x6, local copies, waits for them, and re-layouts, padded_2(): leading = lax.slice_in_dim(value, 0, width, axis=dim)  9.53 us
    reduce_sum x1, other arithmetic, local(): populations.reshape(19, half_x, 2, half_y, 2, half_z, 2)  8.69 us
    slice x4, other arithmetic, from_padded(): padded[i, start[0]:start[0] + sizes[0], start[1]:start[1] + sizes[1], sta...  7.86 us
    broadcast_in_dim x1, local copies, waits for them, and re-layouts, expand_parent(): jnp.broadcast_to(parent[:, :, None, :, None, :, None], (q, a, 2, b, 2, c,...  7.47 us
    another operation x2, local copies, waits for them, and re-layouts, from_padded(): return jnp.stack(moved)  6.27 us
  transfers between devices with their start and end apart: 16, of which 4 were waited for; matrix products, arithmetic and copies ran while one was open for 44% of the time, Pallas kernels for 0%

commit v1 on v0

v1 whole, which is shorter than its diff:
```python
import functools

import jax
import jax.numpy as jnp
import numpy as np
from jax import lax
from jax.experimental import pallas as pl
from jax.experimental.pallas import tpu as pltpu
from jax.sharding import PartitionSpec as P

BIN_Z = 32
VELOCITIES = [
    (0, 0, 0), (1, 0, 0), (-1, 0, 0), (0, 1, 0), (0, -1, 0), (0, 0, 1), (0, 0, -1),
    (1, 1, 0), (-1, -1, 0), (1, -1, 0), (-1, 1, 0), (1, 0, 1), (-1, 0, -1), (1, 0, -1),
    (-1, 0, 1), (0, 1, 1), (0, -1, -1), (0, 1, -1), (0, -1, 1),
]
WEIGHTS = [1.0 / 3.0] + [1.0 / 18.0] * 6 + [1.0 / 36.0] * 12
TAU_FINE = 1.2
TAU_COARSE = 0.85
TO_COARSE = 2.0 * TAU_COARSE / TAU_FINE
TO_FINE = TAU_FINE / (2.0 * TAU_COARSE)
LANES = 128
MESH = pl.DeviceIdType.MESH
SIGNS = (1, -1)
FACE = {(a, s): [i for i in range(19) if VELOCITIES[i][a] == s] for a in range(3) for s in SIGNS}
FACES = [(a, s) for a in range(3) for s in SIGNS]
EDGES = [i for i in range(7, 19)]


def along(vector, c):
    total = None
    for part, sign in zip(vector, c):
        if sign:
            total = part if total is None else (total + part if sign > 0 else total - part)
    return total


def moments(p):
    rho = p[0]
    sums = [None] * 19
    m = [None] * 3
    for i in range(1, 19, 2):
        rho = rho + (p[i] + p[i + 1])
        sums[i] = p[i] - p[i + 1]
        for axis, sign in enumerate(VELOCITIES[i]):
            if sign:
                if m[axis] is None:
                    m[axis] = sums[i]
                else:
                    m[axis] = m[axis] + sums[i] if sign > 0 else m[axis] - sums[i]
    return rho, m


def relax(p, rho, u, a, b, force=None, k=0.0):
    scaled = b * rho
    base = scaled * (1.0 - 1.5 * (u[0] * u[0] + u[1] * u[1] + u[2] * u[2]))
    lin = [3.0 * scaled * v for v in u]
    quad = [4.5 * scaled * v for v in u]
    if force is not None:
        base = base - (3.0 * k) * (u[0] * force[0] + u[1] * force[1] + u[2] * force[2])
        lin = [v + (3.0 * k) * f for v, f in zip(lin, force)]
        quad = [v + (9.0 * k) * f for v, f in zip(quad, force)]
    out = [None] * 19
    out[0] = a * p[0] + WEIGHTS[0] * base
    for i in range(1, 19, 2):
        c, w = VELOCITIES[i], WEIGHTS[i]
        even = w * (base + along(u, c) * along(quad, c))
        odd = w * along(lin, c)
        out[i] = a * p[i] + (even + odd)
        out[i + 1] = a * p[i + 1] + (even - odd)
    return out


def parts(x):
    high = x.astype(jnp.bfloat16)
    return high, (x - high.astype(jnp.float32)).astype(jnp.bfloat16)


def times_exact(x, table):
    high, low = parts(x)
    dot = functools.partial(jnp.dot, preferred_element_type=jnp.float32)
    return dot(high, table) + dot(low, table)


def moved(plane, c):
    rows, lanes = plane.shape
    if c[1]:
        plane = pltpu.roll(plane, 1 if c[1] > 0 else rows - 1, 0)
    if c[2]:
        plane = pltpu.roll(plane, 1 if c[2] > 0 else lanes - 1, 1)
    return plane


def kernel(
    sizes, slots, pop_in, cpop_in, fmask_in, cmask_in, bead_ref, bins_ref, fine_out, coarse_out,
    pops, cpops, fmask, cmask, summed, restricted, parent, wide, tall, force, stream, cstream,
    bead_send, bead_recv, bead_tiles, xs, ys, zs, xr, yr, zr, er_y, er_z,
    in_sem, out_sem, bead_sem, send_sem, recv_sem,
):
    ngx, ngy, ngz = sizes
    gx, gy, gz = lax.axis_index("gx"), lax.axis_index("gy"), lax.axis_index("gz")
    owners = ngx * ngy
    me = gx * ngy + gy
    _, nx, ny, nz = pops.shape
    _, hx, hy, hz = cpops.shape
    chunks = bins_ref.shape[0]
    per = LANES // slots

    loads = [
        pltpu.make_async_copy(src, dst, in_sem.at[n])
        for n, (src, dst) in enumerate(
            ((pop_in, pops), (cpop_in, cpops), (fmask_in, fmask), (cmask_in, cmask))
        )
    ]
    for load in loads:
        load.start()

    def device(offset):
        return (
            lax.rem(gx + (offset[0] + ngx), ngx),
            lax.rem(gy + (offset[1] + ngy), ngy),
            lax.rem(gz + (offset[2] + ngz), ngz),
        )

    def owner(step):
        other = lax.rem(me + step, owners)
        return other, (other // ngy, lax.rem(other, ngy), gz)

    barrier = pltpu.get_barrier_semaphore()
    cross = [(0, 0, 1), (0, 0, -1)] + [VELOCITIES[i] for i in EDGES if VELOCITIES[i][2]]
    for offset in cross:
        pl.semaphore_signal(barrier, inc=1, device_id=device(offset), device_id_type=MESH)

    @pl.loop(1, owners)
    def _(step):
        pl.semaphore_signal(barrier, inc=1, device_id=owner(step)[1], device_id_type=MESH)

    for chunk in range(chunks):
        bead_send[chunk, 0:6, :] = bead_ref[pl.ds(chunk, 6, stride=chunks), :]
        bead_send[chunk, 6:7, :] = bins_ref[chunk : chunk + 1, :].astype(jnp.float32)
        bead_send[chunk, 7:8, :] = jnp.zeros((1, LANES), jnp.float32)
    bead_recv[me] = bead_send[me // per]

    pl.semaphore_wait(barrier, len(cross) + owners - 1)

    @pl.loop(1, owners)
    def _(step):
        other, where = owner(step)
        pltpu.make_async_remote_copy(
            src_ref=bead_send.at[other // per],
            dst_ref=bead_recv.at[me],
            send_sem=bead_sem.at[0],
            recv_sem=bead_sem.at[1],
            device_id=where,
            device_id_type=MESH,
        ).start()

    for load in loads:
        load.wait()

    @pl.loop(0, 19)
    def _(q):
        for x in range(hx):
            total = None
            for i in range(2):
                for j in range(2):
                    piece = pops[q, 2 * x + i, pl.ds(j, hy, stride=2), :]
                    total = piece if total is None else total + piece
            summed[q, x] = total

    fold = lax.broadcasted_iota(jnp.int32, (nz, hz), 0) - 2 * lax.broadcasted_iota(
        jnp.int32, (nz, hz), 1
    )
    fold = jnp.where((fold == 0) | (fold == 1), 0.125, 0.0).astype(jnp.bfloat16)
    restricted[...] = times_exact(summed[...].reshape(19 * hx * hy, nz), fold).reshape(
        19, hx, hy, hz
    )

    @pl.loop(0, hx)
    def _(x):
        p = [restricted[i, x] for i in range(19)]
        rho, m = moments(p)
        inv = 1.0 / rho
        pre = relax(p, rho, [v * inv for v in m], TO_COARSE, 1.0 - TO_COARSE)
        live = cmask[x] == 1
        pre = [jnp.where(live, pre[i], cpops[i, x]) for i in range(19)]
        rho, m = moments(pre)
        inv = 1.0 / rho
        u = [v * inv for v in m]
        down = relax(pre, rho, u, TO_FINE, 1.0 - TO_FINE)
        post = relax(pre, rho, u, 1.0 - 1.0 / TAU_COARSE, 1.0 / TAU_COARSE)
        for i in range(19):
            c = VELOCITIES[i]
            parent[i, x] = down[i]
            cstream[i, lax.rem(x + (c[0] + hx), hx)] = moved(post[i], c)

    spread = lax.broadcasted_iota(jnp.int32, (hz, nz), 1) - 2 * lax.broadcasted_iota(
        jnp.int32, (hz, nz), 0
    )
    spread = jnp.where((spread == 0) | (spread == 1), 1.0, 0.0).astype(jnp.bfloat16)
    wide[...] = times_exact(parent[...].reshape(19 * hx * hy, hz), spread).reshape(19, hx, hy, nz)

    @pl.loop(0, 19)
    def _(q):
        for x in range(hx):
            value = wide[q, x]
            tall[x, pl.ds(0, hy, stride=2), :] = value
            tall[x, pl.ds(1, hy, stride=2), :] = value
        for x in range(nx):
            pops[q, x] = jnp.where(fmask[x] == 1, pops[q, x], tall[x // 2])

    lane_c = lax.broadcasted_iota(jnp.int32, (hy, LANES), 1)
    for a, s in FACES:
        slot = 0 if s > 0 else 1
        if a == 2:
            packed = jnp.zeros((hy, LANES), jnp.float32)
        for j, i in enumerate(FACE[a, s]):
            if a == 0:
                xs[slot, j, ny:, 0:hz] = cstream[i, 0 if s > 0 else hx - 1]
            elif a == 1:
                row = 0 if s > 0 else hy - 1
                for x in range(hx):
                    ys[slot, j, nx + x : nx + x + 1, 0:hz] = cstream[i, x, row : row + 1, :]
            else:
                col = 0 if s > 0 else hz - 1
                for x in range(hx):
                    packed = jnp.where(
                        lane_c == j * hx + x, cstream[i, x, :, col : col + 1], packed
                    )
        if a == 2:
            zs[slot, ny:, :] = packed

    arrived = bead_recv.at[pl.ds(0, owners - 1)]
    pltpu.make_async_copy(arrived, arrived, bead_sem.at[1]).wait()
    lane = lax.broadcasted_iota(jnp.int32, (8, LANES), 1)
    mine = lax.rem(me, per)

    @pl.loop(0, owners // per)
    def _(t):
        tile = jnp.zeros((8, LANES), jnp.float32)
        for k in range(per):
            turned = pltpu.roll(
                bead_recv[t * per + k], lax.rem((k + per - mine) * slots, LANES), 1
            )
            tile = jnp.where((lane >= k * slots) & (lane < (k + 1) * slots), turned, tile)
        bead_tiles[t] = tile

    force[...] = jnp.zeros_like(force)
    bins_y, bins_z = ny // 2, nz // BIN_Z

    def window(start, position, live, cells, span):
        offset = lax.broadcasted_iota(jnp.int32, (cells, LANES), 0).astype(jnp.float32) - start
        distance = offset - position
        inside = (offset >= 0.0) & (offset < span) & live
        return jnp.where(inside, jnp.exp(-0.5 * distance * distance), 0.0)

    @pl.loop(0, owners // per)
    def _(t):
        tile = bead_tiles[t]
        number = tile[6:7]
        live = number >= 0.0
        bx = jnp.floor((number + 0.5) * (1.0 / (bins_y * bins_z)))
        rest = number - bx * (bins_y * bins_z)
        by = jnp.floor((rest + 0.5) * (1.0 / bins_z))
        bz = rest - by * bins_z
        wx = window(2.0 * bx, tile[0:1], live, nx, 2.0)
        wy = window(2.0 * by, tile[1:2], live, ny, 2.0)
        wz = window(float(BIN_Z) * bz, tile[2:3], live, nz, float(BIN_Z))
        rows = []
        for d in range(3):
            pushed = wx * tile[3 + d : 4 + d]
            for x in range(nx):
                rows.append(pushed[x : x + 1] * wy)
        left = jnp.concatenate(rows, axis=0)
        lh, ll = parts(left)
        rh, rl = parts(wz)
        total = lax.dot_general(
            jnp.concatenate([lh, lh, ll], axis=1),
            jnp.concatenate([rh, rl, rh], axis=1),
            (((1,), (1,)), ((), ())),
            preferred_element_type=jnp.float32,
        )
        force[...] += total.reshape(3, nx, ny, nz)

    @pl.loop(0, nx)
    def _(x):
        p = [pops[i, x] for i in range(19)]
        f = [force[d, x] for d in range(3)]
        rho, m = moments(p)
        inv = 1.0 / rho
        u = [(v + 0.5 * w) * inv for v, w in zip(m, f)]
        post = relax(
            p, rho, u, 1.0 - 1.0 / TAU_FINE, 1.0 / TAU_FINE, f, 1.0 - 0.5 / TAU_FINE
        )
        for i in range(19):
            c = VELOCITIES[i]
            stream[i, lax.rem(x + (c[0] + nx), nx)] = moved(post[i], c)

    lane_f = lax.broadcasted_iota(jnp.int32, (ny, LANES), 1)
    for a, s in FACES:
        slot = 0 if s > 0 else 1
        for j, i in enumerate(FACE[a, s]):
            if a == 0:
                xs[slot, j, 0:ny, :] = stream[i, 0 if s > 0 else nx - 1]
            elif a == 1:
                row = 0 if s > 0 else ny - 1
                for x in range(nx):
                    ys[slot, j, x : x + 1, :] = stream[i, x, row : row + 1, :]
        if a == 2:
            col = 0 if s > 0 else nz - 1

            def pack(x, packed):
                for j, i in enumerate(FACE[a, s]):
                    packed = jnp.where(
                        lane_f == j * nx + x, stream[i, x, :, col : col + 1], packed
                    )
                return packed

            zs[slot, 0:ny, :] = lax.fori_loop(0, nx, pack, jnp.zeros((ny, LANES), jnp.float32))

    copies = []

    def send(src, dst, offset):
        n = len(copies)
        copy = pltpu.make_async_remote_copy(
            src_ref=src, dst_ref=dst, send_sem=send_sem.at[n], recv_sem=recv_sem.at[n],
            device_id=device(offset), device_id_type=MESH,
        )
        copy.start()
        copies.append(copy)

    for a, s in FACES:
        slot = 0 if s > 0 else 1
        offset = tuple(s if axis == a else 0 for axis in range(3))
        src, dst = ((xs, xr), (ys, yr), (zs, zr))[a]
        send(src.at[slot], dst.at[slot], offset)
    for n, i in enumerate(EDGES):
        c = VELOCITIES[i]
        if c[2]:
            send(zs.at[0 if c[2] > 0 else 1], er_z.at[n - 4], c)
        else:
            slot = 0 if c[1] > 0 else 1
            send(ys.at[slot, FACE[1, c[1]].index(i)], er_y.at[n], c)
    pltpu.make_async_copy(arrived, arrived, bead_sem.at[0]).wait()
    for copy in copies:
        copy.wait()

    def side(sign, length):
        return 0 if sign > 0 else length - 1

    for target, rows_y, shape in (
        (stream, slice(0, ny), (nx, ny, nz)),
        (cstream, slice(ny, ny + hy), (hx, hy, hz)),
    ):
        fx, fy, fz = shape
        first = 0 if target is stream else nx
        low = 0 if target is stream else ny
        lane_t = lax.broadcasted_iota(jnp.int32, (fy, LANES), 1)
        row_t = lax.broadcasted_iota(jnp.int32, (fy, LANES), 0)
        for s in SIGNS:
            for j, i in enumerate(FACE[0, s]):
                target[i, side(s, fx)] = xr[0 if s > 0 else 1, j, rows_y, 0:fz]
        for s in SIGNS:
            for j, i in enumerate(FACE[1, s]):
                c = VELOCITIES[i]
                y = side(s, fy)
                for x in range(fx):
                    src = yr.at[0 if s > 0 else 1, j]
                    if c[0] and x == side(c[0], fx):
                        src = er_y.at[EDGES.index(i)]
                    target[i, x, y : y + 1, :] = src[first + x : first + x + 1, 0:fz]
        for s in SIGNS:
            column = zr[0 if s > 0 else 1, low : low + fy, :]
            for j, i in enumerate(FACE[2, s]):
                c = VELOCITIES[i]
                if c[0]:
                    spot = lane_t == j * fx + side(c[0], fx)
                elif c[1]:
                    spot = (
                        (lane_t >= j * fx) & (lane_t < (j + 1) * fx) & (row_t == side(c[1], fy))
                    )
                else:
                    continue
                column = jnp.where(spot, er_z[EDGES.index(i) - 4, low : low + fy, :], column)
            edge = lax.broadcasted_iota(jnp.int32, (fy, fz), 1) == side(s, fz)
            for j, i in enumerate(FACE[2, s]):
                for x in range(fx):
                    k = j * fx + x
                    target[i, x] = jnp.where(edge, column[:, k : k + 1], target[i, x])

    stores = [
        pltpu.make_async_copy(stream, fine_out, out_sem.at[0]),
        pltpu.make_async_copy(cstream, coarse_out, out_sem.at[1]),
    ]
    for store in stores:
        store.start()
    for store in stores:
        store.wait()


def local(populations, coarse_pops, fine_mask, coarse_mask, bead_data, bead_bins):
    _, nx, ny, nz = populations.shape
    _, hx, hy, hz = coarse_pops.shape
    sizes = tuple(lax.axis_size(axis) for axis in ("gx", "gy", "gz"))
    owners = sizes[0] * sizes[1]
    total = bead_data.shape[4]
    chunks = total // LANES
    slots = total // owners
    beads = bead_data.reshape(6 * chunks, LANES)
    bins = bead_bins.reshape(chunks, LANES)
    f32, i32 = jnp.float32, jnp.int32
    rows = nx + 8 * ((hx + 7) // 8)
    any_spec = pl.BlockSpec(memory_space=pl.ANY)
    vmem_spec = pl.BlockSpec(memory_space=pltpu.VMEM)
    dma = pltpu.SemaphoreType.DMA
    return pl.pallas_call(
        functools.partial(kernel, sizes, slots),
        out_shape=(
            jax.ShapeDtypeStruct(populations.shape, f32),
            jax.ShapeDtypeStruct(coarse_pops.shape, f32),
        ),
        in_specs=[any_spec] * 4 + [vmem_spec] * 2,
        out_specs=(any_spec, any_spec),
        scratch_shapes=[
            pltpu.VMEM((19, nx, ny, nz), f32),
            pltpu.VMEM((19, hx, hy, hz), f32),
            pltpu.VMEM((nx, ny, nz), i32),
            pltpu.VMEM((hx, hy, hz), i32),
            pltpu.VMEM((19, hx, hy, nz), f32),
            pltpu.VMEM((19, hx, hy, hz), f32),
            pltpu.VMEM((19, hx, hy, hz), f32),
            pltpu.VMEM((19, hx, hy, nz), f32),
            pltpu.VMEM((hx, ny, nz), f32),
            pltpu.VMEM((3, nx, ny, nz), f32),
            pltpu.VMEM((19, nx, ny, nz), f32),
            pltpu.VMEM((19, hx, hy, hz), f32),
            pltpu.VMEM((chunks, 8, LANES), f32),
            pltpu.VMEM((owners, 8, LANES), f32),
            pltpu.VMEM((total // LANES, 8, LANES), f32),
            pltpu.VMEM((2, 5, ny + hy, LANES), f32),
            pltpu.VMEM((2, 5, rows, LANES), f32),
            pltpu.VMEM((2, ny + hy, LANES), f32),
            pltpu.VMEM((2, 5, ny + hy, LANES), f32),
            pltpu.VMEM((2, 5, rows, LANES), f32),
            pltpu.VMEM((2, ny + hy, LANES), f32),
            pltpu.VMEM((4, rows, LANES), f32),
            pltpu.VMEM((8, ny + hy, LANES), f32),
            dma((4,)),
            dma((2,)),
            dma((2,)),
            dma((18,)),
            dma((18,)),
        ],
        compiler_params=pltpu.CompilerParams(collective_id=0, has_side_effects=True),
    )(populations, coarse_pops, fine_mask, coarse_mask, beads, bins)


def solution(mesh):
    in_specs = (
        P(None, "gx", "gy", "gz"),
        P(None, "gx", "gy", "gz"),
        P("gx", "gy", "gz"),
        P("gx", "gy", "gz"),
        P("gx", "gy", "gz", None, None),
        P("gx", "gy", "gz", None, None),
    )
    out_specs = (P(None, "gx", "gy", "gz"), P(None, "gx", "gy", "gz"))
    return jax.shard_map(local, mesh=mesh, in_specs=in_specs, out_specs=out_specs, check_vma=False)
```

time: 143 us -> 27.7 us (0.19)
  local copies, waits for them, and re-layouts: 55 us -> 3.21 us
  starting transfers between devices: 31.9 us -> 0 us
  other arithmetic: 31.8 us -> 0 us
  Pallas kernels: 0 us -> 23.6 us
  matrix products: 11.7 us -> 0 us
  waiting for transfers between devices: 10 us -> 0 us
    pallas_call x0 -> x1, Pallas kernels: none -> 23.6 us  [local(): pl.pallas_call(functools.partial(kernel, sizes, slots), out_shape=(jax.Sh...]
    ppermute x12 -> x0, starting transfers between devices: 16 us -> none  [the longest x6 11.3 us: padded_2(): after = lax.ppermute(leading, axis, down)]
    all_to_all x4 -> x0, starting transfers between devices: 15.9 us -> none  [the longest x1 5.96 us: local(): lax.all_to_all(sectioned, 'gx', split_axis=4, concat_axis=4, tiled=True)]
    slice x15 -> x0, local copies, waits for them, and re-layouts: 13.5 us -> none  [the longest x6 9.53 us: padded_2(): leading = lax.slice_in_dim(value, 0, width, axis=dim)]
    dot_general x8 -> x0, matrix products: 11.7 us -> none  [the longest x3 5.15 us: equilibrium(): jnp.tensordot(table, velocity, axes=1, precision=lax.Precision.HIGHEST)]
    reduce_sum x3 -> x0, other arithmetic: 9.84 us -> none  [the longest x1 8.69 us: local(): populations.reshape(19, half_x, 2, half_y, 2, half_z, 2)]
    concatenate x10 -> x0, other arithmetic: 9.82 us -> none  [padded_2(): value = jnp.concatenate([before, value, after], axis=dim)]
    all_to_all x4 -> x0, waiting for transfers between devices: 9.29 us -> none  [the longest x1 4.7 us: local(): lax.all_to_all(sectioned, 'gx', split_axis=4, concat_axis=4, tiled=True)]
  transfers between devices with their start and end apart: 16 -> 0, of which waited for: 4 -> 0; matrix products, arithmetic and copies ran while one was open for 44% -> 0% of each run, Pallas kernels for 0% -> 0%
where the time goes in v1:
time: 27.7 us; the launch traced here: 27.4 us
  Pallas kernels  23.6 us (85%)
  local copies, waits for them, and re-layouts  3.21 us (12%)
  between operations  0.65 us (2%)
    pallas_call x1, Pallas kernels, local(): pl.pallas_call(functools.partial(kernel, sizes, slots), out_shape=(jax.Sh...  23.6 us
    unnamed x4, local copies, waits for them, and re-layouts  3.21 us

profile of v1, /device:TPU:0, one launch (start us, length us, event | category | flops | bytes accessed | tf_op | source)
XLA Modules:
  0.0 27.4 jit_solution(542803012763712800)
XLA Ops:
  0.6 23.6 %shard_map.77 = (f32[19,8,16,128]{3,2,1,0:T(8,128)}, f32[19,4,8,64]{3,2,1,0:T(8,128)}) custom-call(f32[19,8,16,128]{3,2,1,0:T(8,128)} %pop_in.1, f32[19,4,8,64]{3,2,1,0:T(8,128)} %cpop_in.1, s32[8,16,128]{2,1,0:T(8,128)} %fmask_in.1, s32[4,8,64]{2,1,0:T(8,128)} %cmask_in.1, f32[24,128]{1,0:T(8,128)} %bitcast.2, s32[4,128]{1,0:T(4,128)} %bitcast.3), custom_call_target="tpu_custom_call" | custom-call | tf_op jit(solution)/shard_map/pallas_call | solution.py:416
  24.2 0.0 copy-start
  24.2 2.5 %copy.10 = f32[19,8,16,128]{3,2,1,0:T(8,128)} copy(f32[19,8,16,128]{3,2,1,0:T(8,128)} %get-tuple-element.4) | data formatting | bytes 2490368
  26.7 0.0 copy-done
  26.7 0.7 %copy.11 = f32[19,4,8,64]{3,2,1,0:T(8,128)} copy(f32[19,4,8,64]{3,2,1,0:T(8,128)S(1)} %copy-done) | data formatting | bytes 311296
Async XLA Ops:
  24.2 2.5 %copy-start = (f32[19,4,8,64]{3,2,1,0:T(8,128)S(1)}, f32[19,4,8,64]{3,2,1,0:T(8,128)}, u32[]{:S(2)}) copy-start(f32[19,4,8,64]{3,2,1,0:T(8,128)} %get-tuple-element.5) | copy-start | bytes 466948

commit v2 on v1

--- a/solution.py
+++ b/solution.py
@@ -20,6 +20,7 @@
 TO_COARSE = 2.0 * TAU_COARSE / TAU_FINE
 TO_FINE = TAU_FINE / (2.0 * TAU_COARSE)
 LANES = 128
+LIMIT = 24 * 2**20
 MESH = pl.DeviceIdType.MESH
 SIGNS = (1, -1)
 FACE = {(a, s): [i for i in range(19) if VELOCITIES[i][a] == s] for a in range(3) for s in SIGNS}
@@ -91,11 +92,110 @@
     return plane
 
 
+def side(sign, length):
+    return 0 if sign > 0 else length - 1
+
+
+def slot_of(sign):
+    return 0 if sign > 0 else 1
+
+
+def pack_x(target, xs, es):
+    _, fx, fy, fz = target.shape
+    row = lax.broadcasted_iota(jnp.int32, (fy, LANES), 0)
+    diagonal = row == lax.broadcasted_iota(jnp.int32, (fy, LANES), 1)
+    for s in SIGNS:
+        for j, i in enumerate(FACE[0, s]):
+            plane = target[i, side(s, fx)]
+            xs[slot_of(s), j] = plane
+            c = VELOCITIES[i]
+            if c[1]:
+                y = side(c[1], fy)
+                es[EDGES.index(i), :, 0:fz] = plane[y : y + 1]
+            elif c[2]:
+                z = side(c[2], fz)
+                turned = jnp.where(diagonal, plane[:, z : z + 1], 0.0)
+                es[EDGES.index(i)] = jnp.sum(turned, axis=0, keepdims=True)
+
+
+def pack_yz(target, ys, zs, es):
+    _, fx, fy, fz = target.shape
+    lane = lax.broadcasted_iota(jnp.int32, (fy, LANES), 1)
+    for s in SIGNS:
+        y, z = side(s, fy), side(s, fz)
+        for j, i in enumerate(FACE[1, s]):
+            for x in range(fx):
+                ys[slot_of(s), j * fx + x : j * fx + x + 1, :] = target[i, x, y : y + 1, :]
+        packed = jnp.zeros((fy, LANES), jnp.float32)
+        for j, i in enumerate(FACE[2, s]):
+            for x in range(fx):
+                packed = jnp.where(lane == j * fx + x, target[i, x, :, z : z + 1], packed)
+        zs[slot_of(s)] = packed
+        for i in FACE[2, s]:
+            c = VELOCITIES[i]
+            if c[1]:
+                y = side(c[1], fy)
+                es[EDGES.index(i)] = packed[y : y + 1]
+
+
+def finish(*refs):
+    levels = (refs[0:5], refs[5:10])
+    outs, targets, store_sem = refs[10:12], refs[12:14], refs[14]
+    stores = []
+    for n in (0, 1):
+        target = targets[n]
+        source, xr, yr, zr, er = levels[n]
+        _, fx, fy, fz = target.shape
+        lane = lax.broadcasted_iota(jnp.int32, (fy, LANES), 1)
+        row = lax.broadcasted_iota(jnp.int32, (fy, LANES), 0)
+        last = lax.broadcasted_iota(jnp.int32, (fy, fz), 1)
+        columns = []
+        for s in SIGNS:
+            column = zr[slot_of(s)]
+            for j, i in enumerate(FACE[2, s]):
+                c = VELOCITIES[i]
+                if c[0]:
+                    value = jnp.sum(
+                        jnp.where(row == lane, er[EDGES.index(i)], 0.0), axis=1, keepdims=True
+                    )
+                    column = jnp.where(lane == j * fx + side(c[0], fx), value, column)
+                elif c[1]:
+                    spot = (lane >= j * fx) & (lane < (j + 1) * fx) & (row == side(c[1], fy))
+                    column = jnp.where(spot, er[EDGES.index(i)], column)
+            columns.append(column)
+        for i in range(19):
+            c = VELOCITIES[i]
+            target[i] = source[i]
+            if c[0]:
+                target[i, side(c[0], fx)] = xr[slot_of(c[0]), FACE[0, c[0]].index(i)]
+            if c[1]:
+                y, j = side(c[1], fy), FACE[1, c[1]].index(i)
+                for x in range(fx):
+                    if c[0] and x == side(c[0], fx):
+                        piece = er[EDGES.index(i), :, 0:fz]
+                    else:
+                        piece = yr[slot_of(c[1]), j * fx + x : j * fx + x + 1, :]
+                    target[i, x, y : y + 1, :] = piece
+            if c[2]:
+                j, column = FACE[2, c[2]].index(i), columns[slot_of(c[2])]
+                for x in range(fx):
+                    k = j * fx + x
+                    target[i, x] = jnp.where(
+                        last == side(c[2], fz), column[:, k : k + 1], target[i, x]
+                    )
+            store = pltpu.make_async_copy(target.at[i], outs[n].at[i], store_sem.at[n, i])
+            store.start()
+            stores.append(store)
+    for store in stores:
+        store.wait()
+
+
 def kernel(
-    sizes, slots, pop_in, cpop_in, fmask_in, cmask_in, bead_ref, bins_ref, fine_out, coarse_out,
-    pops, cpops, fmask, cmask, summed, restricted, parent, wide, tall, force, stream, cstream,
-    bead_send, bead_recv, bead_tiles, xs, ys, zs, xr, yr, zr, er_y, er_z,
-    in_sem, out_sem, bead_sem, send_sem, recv_sem,
+    sizes, slots, pop_in, cpop_in, fmask_in, cmask_in, bead_ref, bins_ref,
+    stream, fxr, fyr, fzr, fer, cstream, cxr, cyr, czr, cer,
+    pops, cpops, fmask, cmask, summed, restricted, parent, wide, tall, force,
+    bead_send, bead_recv, bead_tiles, fxs, fys, fzs, fes, cxs, cys, czs, ces,
+    in_sem, bead_sem, send_sem, recv_sem,
 ):
     ngx, ngy, ngz = sizes
     gx, gy, gz = lax.axis_index("gx"), lax.axis_index("gy"), lax.axis_index("gz")
@@ -126,12 +226,19 @@
         other = lax.rem(me + step, owners)
         return other, (other // ngy, lax.rem(other, ngy), gz)
 
+    def each_peer(act):
+        if owners > 32:
+            pl.loop(1, owners)(act)
+        else:
+            for step in sorted(range(1, owners), key=lambda n: -min(n, owners - n)):
+                act(step)
+
     barrier = pltpu.get_barrier_semaphore()
     cross = [(0, 0, 1), (0, 0, -1)] + [VELOCITIES[i] for i in EDGES if VELOCITIES[i][2]]
     for offset in cross:
         pl.semaphore_signal(barrier, inc=1, device_id=device(offset), device_id_type=MESH)
 
-    @pl.loop(1, owners)
+    @each_peer
     def _(step):
         pl.semaphore_signal(barrier, inc=1, device_id=owner(step)[1], device_id_type=MESH)
 
@@ -143,7 +250,7 @@
 
     pl.semaphore_wait(barrier, len(cross) + owners - 1)
 
-    @pl.loop(1, owners)
+    @each_peer
     def _(step):
         other, where = owner(step)
         pltpu.make_async_remote_copy(
@@ -209,26 +316,36 @@
         for x in range(nx):
             pops[q, x] = jnp.where(fmask[x] == 1, pops[q, x], tall[x // 2])
 
-    lane_c = lax.broadcasted_iota(jnp.int32, (hy, LANES), 1)
-    for a, s in FACES:
-        slot = 0 if s > 0 else 1
-        if a == 2:
-            packed = jnp.zeros((hy, LANES), jnp.float32)
-        for j, i in enumerate(FACE[a, s]):
-            if a == 0:
-                xs[slot, j, ny:, 0:hz] = cstream[i, 0 if s > 0 else hx - 1]
-            elif a == 1:
-                row = 0 if s > 0 else hy - 1
-                for x in range(hx):
-                    ys[slot, j, nx + x : nx + x + 1, 0:hz] = cstream[i, x, row : row + 1, :]
-            else:
-                col = 0 if s > 0 else hz - 1
-                for x in range(hx):
-                    packed = jnp.where(
-                        lane_c == j * hx + x, cstream[i, x, :, col : col + 1], packed
-                    )
-        if a == 2:
-            zs[slot, ny:, :] = packed
+    copies = []
+
+    def send(src, dst, offset):
+        n = len(copies)
+        copy = pltpu.make_async_remote_copy(
+            src_ref=src, dst_ref=dst, send_sem=send_sem.at[n], recv_sem=recv_sem.at[n],
+            device_id=device(offset), device_id_type=MESH,
+        )
+        copy.start()
+        copies.append(copy)
+
+    def send_x(xs, xr, es, er):
+        for s in SIGNS:
+            send(xs.at[slot_of(s)], xr.at[slot_of(s)], (s, 0, 0))
+        for n, i in enumerate(EDGES):
+            if VELOCITIES[i][0]:
+                send(es.at[n], er.at[n], VELOCITIES[i])
+
+    def send_yz(ys, yr, zs, zr, es, er):
+        for s in SIGNS:
+            send(ys.at[slot_of(s)], yr.at[slot_of(s)], (0, s, 0))
+            send(zs.at[slot_of(s)], zr.at[slot_of(s)], (0, 0, s))
+        for n, i in enumerate(EDGES):
+            if not VELOCITIES[i][0]:
+                send(es.at[n], er.at[n], VELOCITIES[i])
+
+    pack_x(cstream, cxs, ces)
+    send_x(cxs, cxr, ces, cer)
+    pack_yz(cstream, cys, czs, ces)
+    send_yz(cys, cyr, czs, czr, ces, cer)
 
     arrived = bead_recv.at[pl.ds(0, owners - 1)]
     pltpu.make_async_copy(arrived, arrived, bead_sem.at[1]).wait()
@@ -282,8 +399,8 @@
         )
         force[...] += total.reshape(3, nx, ny, nz)
 
-    @pl.loop(0, nx)
-    def _(x):
+    def collide(k):
+        x = lax.rem(k + (nx - 1), nx)
         p = [pops[i, x] for i in range(19)]
         f = [force[d, x] for d in range(3)]
         rho, m = moments(p)
@@ -296,106 +413,15 @@
             c = VELOCITIES[i]
             stream[i, lax.rem(x + (c[0] + nx), nx)] = moved(post[i], c)
 
-    lane_f = lax.broadcasted_iota(jnp.int32, (ny, LANES), 1)
-    for a, s in FACES:
-        slot = 0 if s > 0 else 1
-        for j, i in enumerate(FACE[a, s]):
-            if a == 0:
-                xs[slot, j, 0:ny, :] = stream[i, 0 if s > 0 else nx - 1]
-            elif a == 1:
-                row = 0 if s > 0 else ny - 1
-                for x in range(nx):
-                    ys[slot, j, x : x + 1, :] = stream[i, x, row : row + 1, :]
-        if a == 2:
-            col = 0 if s > 0 else nz - 1
-
-            def pack(x, packed):
-                for j, i in enumerate(FACE[a, s]):
-                    packed = jnp.where(
-                        lane_f == j * nx + x, stream[i, x, :, col : col + 1], packed
-                    )
-                return packed
-
-            zs[slot, 0:ny, :] = lax.fori_loop(0, nx, pack, jnp.zeros((ny, LANES), jnp.float32))
-
-    copies = []
-
-    def send(src, dst, offset):
-        n = len(copies)
-        copy = pltpu.make_async_remote_copy(
-            src_ref=src, dst_ref=dst, send_sem=send_sem.at[n], recv_sem=recv_sem.at[n],
-            device_id=device(offset), device_id_type=MESH,
-        )
-        copy.start()
-        copies.append(copy)
-
-    for a, s in FACES:
-        slot = 0 if s > 0 else 1
-        offset = tuple(s if axis == a else 0 for axis in range(3))
-        src, dst = ((xs, xr), (ys, yr), (zs, zr))[a]
-        send(src.at[slot], dst.at[slot], offset)
-    for n, i in enumerate(EDGES):
-        c = VELOCITIES[i]
-        if c[2]:
-            send(zs.at[0 if c[2] > 0 else 1], er_z.at[n - 4], c)
-        else:
-            slot = 0 if c[1] > 0 else 1
-            send(ys.at[slot, FACE[1, c[1]].index(i)], er_y.at[n], c)
+    pl.loop(0, 2)(collide)
+    pack_x(stream, fxs, fes)
+    send_x(fxs, fxr, fes, fer)
+    pl.loop(2, nx)(collide)
+    pack_yz(stream, fys, fzs, fes)
+    send_yz(fys, fyr, fzs, fzr, fes, fer)
     pltpu.make_async_copy(arrived, arrived, bead_sem.at[0]).wait()
     for copy in copies:
         copy.wait()
-
-    def side(sign, length):
-        return 0 if sign > 0 else length - 1
-
-    for target, rows_y, shape in (
-        (stream, slice(0, ny), (nx, ny, nz)),
-        (cstream, slice(ny, ny + hy), (hx, hy, hz)),
-    ):
-        fx, fy, fz = shape
-        first = 0 if target is stream else nx
-        low = 0 if target is stream else ny
-        lane_t = lax.broadcasted_iota(jnp.int32, (fy, LANES), 1)
-        row_t = lax.broadcasted_iota(jnp.int32, (fy, LANES), 0)
-        for s in SIGNS:
-            for j, i in enumerate(FACE[0, s]):
-                target[i, side(s, fx)] = xr[0 if s > 0 else 1, j, rows_y, 0:fz]
-        for s in SIGNS:
-            for j, i in enumerate(FACE[1, s]):
-                c = VELOCITIES[i]
-                y = side(s, fy)
-                for x in range(fx):
-                    src = yr.at[0 if s > 0 else 1, j]
-                    if c[0] and x == side(c[0], fx):
-                        src = er_y.at[EDGES.index(i)]
-                    target[i, x, y : y + 1, :] = src[first + x : first + x + 1, 0:fz]
-        for s in SIGNS:
-            column = zr[0 if s > 0 else 1, low : low + fy, :]
-            for j, i in enumerate(FACE[2, s]):
-                c = VELOCITIES[i]
-                if c[0]:
-                    spot = lane_t == j * fx + side(c[0], fx)
-                elif c[1]:
-                    spot = (
-                        (lane_t >= j * fx) & (lane_t < (j + 1) * fx) & (row_t == side(c[1], fy))
-                    )
-                else:
-                    continue
-                column = jnp.where(spot, er_z[EDGES.index(i) - 4, low : low + fy, :], column)
-            edge = lax.broadcasted_iota(jnp.int32, (fy, fz), 1) == side(s, fz)
-            for j, i in enumerate(FACE[2, s]):
-                for x in range(fx):
-                    k = j * fx + x
-                    target[i, x] = jnp.where(edge, column[:, k : k + 1], target[i, x])
-
-    stores = [
-        pltpu.make_async_copy(stream, fine_out, out_sem.at[0]),
-        pltpu.make_async_copy(cstream, coarse_out, out_sem.at[1]),
-    ]
-    for store in stores:
-        store.start()
-    for store in stores:
-        store.wait()
 
 
 def local(populations, coarse_pops, fine_mask, coarse_mask, bead_data, bead_bins):
@@ -409,18 +435,21 @@
     beads = bead_data.reshape(6 * chunks, LANES)
     bins = bead_bins.reshape(chunks, LANES)
     f32, i32 = jnp.float32, jnp.int32
-    rows = nx + 8 * ((hx + 7) // 8)
     any_spec = pl.BlockSpec(memory_space=pl.ANY)
+    hbm_spec = pl.BlockSpec(memory_space=pltpu.HBM)
     vmem_spec = pl.BlockSpec(memory_space=pltpu.VMEM)
     dma = pltpu.SemaphoreType.DMA
-    return pl.pallas_call(
+
+    def rim(fx, fy, fz):
+        return [(2, 5, fy, fz), (2, 5 * fx, fz), (2, fy, LANES), (12, 1, LANES)]
+
+    fine_rim, coarse_rim = rim(nx, ny, nz), rim(hx, hy, hz)
+    shapes = [populations.shape, *fine_rim, coarse_pops.shape, *coarse_rim]
+    pieces = pl.pallas_call(
         functools.partial(kernel, sizes, slots),
-        out_shape=(
-            jax.ShapeDtypeStruct(populations.shape, f32),
-            jax.ShapeDtypeStruct(coarse_pops.shape, f32),
-        ),
-        in_specs=[any_spec] * 4 + [vmem_spec] * 2,
-        out_specs=(any_spec, any_spec),
+        out_shape=[jax.ShapeDtypeStruct(shape, f32) for shape in shapes],
+        in_specs=[hbm_spec] * 4 + [vmem_spec] * 2,
+        out_specs=([vmem_spec] + [any_spec] * 4) * 2,
         scratch_shapes=[
             pltpu.VMEM((19, nx, ny, nz), f32),
             pltpu.VMEM((19, hx, hy, hz), f32),
@@ -432,27 +461,36 @@
             pltpu.VMEM((19, hx, hy, nz), f32),
             pltpu.VMEM((hx, ny, nz), f32),
             pltpu.VMEM((3, nx, ny, nz), f32),
-            pltpu.VMEM((19, nx, ny, nz), f32),
-            pltpu.VMEM((19, hx, hy, hz), f32),
             pltpu.VMEM((chunks, 8, LANES), f32),
             pltpu.VMEM((owners, 8, LANES), f32),
             pltpu.VMEM((total // LANES, 8, LANES), f32),
-            pltpu.VMEM((2, 5, ny + hy, LANES), f32),
-            pltpu.VMEM((2, 5, rows, LANES), f32),
-            pltpu.VMEM((2, ny + hy, LANES), f32),
-            pltpu.VMEM((2, 5, ny + hy, LANES), f32),
-            pltpu.VMEM((2, 5, rows, LANES), f32),
-            pltpu.VMEM((2, ny + hy, LANES), f32),
-            pltpu.VMEM((4, rows, LANES), f32),
-            pltpu.VMEM((8, ny + hy, LANES), f32),
+            *[pltpu.VMEM(shape, f32) for shape in fine_rim + coarse_rim],
             dma((4,)),
             dma((2,)),
-            dma((2,)),
-            dma((18,)),
-            dma((18,)),
+            dma((36,)),
+            dma((36,)),
         ],
-        compiler_params=pltpu.CompilerParams(collective_id=0, has_side_effects=True),
-    )(populations, coarse_pops, fine_mask, coarse_mask, beads, bins)
+        compiler_params=pltpu.CompilerParams(
+            collective_id=0, has_side_effects=True, vmem_limit_bytes=LIMIT
+        ),
+    )(*[pltpu.with_memory_space_constraint(v, pltpu.HBM) for v in (populations, coarse_pops, fine_mask, coarse_mask, beads, bins)])
+    return tuple(
+        pl.pallas_call(
+            finish,
+            out_shape=[
+                jax.ShapeDtypeStruct(populations.shape, f32),
+                jax.ShapeDtypeStruct(coarse_pops.shape, f32),
+            ],
+            in_specs=[vmem_spec] * len(shapes),
+            out_specs=[any_spec] * 2,
+            scratch_shapes=[
+                pltpu.VMEM(populations.shape, f32),
+                pltpu.VMEM(coarse_pops.shape, f32),
+                dma((2, 19)),
+            ],
+            compiler_params=pltpu.CompilerParams(vmem_limit_bytes=LIMIT),
+        )(*pieces)
+    )
 
 
 def solution(mesh):

time: 27.7 us -> 22.7 us (0.82)
  local copies, waits for them, and re-layouts: 3.21 us -> 0 us
  Pallas kernels: 23.6 us -> 21.8 us
    unnamed x4 -> x0, local copies, waits for them, and re-layouts: 3.21 us -> none
    pallas_call x1 -> x2, Pallas kernels: 23.6 us -> 21.8 us  [the longest x1 20.2 us: local(): pl.pallas_call(functools.partial(kernel, sizes, slots), out_shape=[jax.Sh...]
where the time goes in v2:
time: 22.7 us; the launch traced here: 22.4 us
  Pallas kernels  21.8 us (96%)
  between operations  0.64 us (3%)
    pallas_call x1, Pallas kernels, local(): pl.pallas_call(functools.partial(kernel, sizes, slots), out_shape=[jax.Sh...  20.2 us
    pallas_call x1, Pallas kernels, local(): pl.pallas_call(finish, out_shape=[jax.ShapeDtypeStruct(populations.shape,...  1.57 us

profile of v2, /device:TPU:0, one launch (start us, length us, event | category | flops | bytes accessed | tf_op | source)
XLA Modules:
  0.0 22.4 jit_solution(241790116698572201)
XLA Ops:
  0.6 20.2 %shard_map.77 = (f32[19,8,16,128]{3,2,1,0:T(8,128)S(1)}, f32[2,5,16,128]{3,2,1,0:T(8,128)S(1)}, f32[2,40,128]{2,1,0:T(8,128)S(1)}, f32[2,16,128]{2,1,0:T(8,128)S...) custom-call(f32[19,8,16,128]{3,2,1,0:T(8,128)} %pop_in.1, ...), custom_call_target="tpu_custom_call" | custom-call | tf_op jit(solution)/shard_map/pallas_call | solution.py:448
  20.9 1.6 %shard_map.78 = (f32[19,8,16,128]{3,2,1,0:T(8,128)}, f32[19,4,8,64]{3,2,1,0:T(8,128)}) custom-call(f32[19,8,16,128]{3,2,1,0:T(8,128)S(1)} %get-tuple-element.12.refs_0_, f32[2,5,16,128]{3,2,1,0:T(8,128)S(1)} %get-tuple-element.13.refs_1_, f32[2,40,128]{2,1,0:T(8,128)S(1)} %get-tuple-element.14.refs_2_, f32[2,16,128]{2,1,0:T(8,128)S(1)} %get-tuple-element.15.refs_3_, ...), custom_call_target="tpu_custom_call" | custom-call | tf_op jit(solution)/shard_map/pallas_call | solution.py:478
